TPU v7x, 512 devices: a whole 4x8x8 slice. The times are simulated.
512 devices in a mesh: dp: 16 (over z, core), expert: 32 (over x, y).
Axes of the slice: x: 4, y: 8, z: 8, core: 2. Of those that a mesh axis runs over, the one named last changes fastest.
Arguments:
- tokens: bfloat16 [65536, 1664], P(('dp', 'expert')), may hold values from -6 to 6
- cotangent: bfloat16 [65536, 1664], P(('dp', 'expert')), may hold values from -6 to 6
- counts: int32 [65536], P(('dp', 'expert')), may hold values from 0 to 8
- picks: int32 [16, 32, 32], P('dp'), may hold values from 0 to 4095, as said below
- router: float32 [1664, 32], replicated, may hold values from -1 to 1
- w_in: bfloat16 [32, 1664, 4096], P('expert', None, 'dp'), may hold values from -0.15625 to 0.15625
- w_out: bfloat16 [32, 4096, 1664], P('expert', 'dp'), may hold values from -0.09375 to 0.09375
Outputs:
- grad_tokens: bfloat16 [65536, 1664], P(('dp', 'expert'))
- grad_w_in: bfloat16 [32, 1664, 4096], P('expert', None, 'dp')
- grad_w_out: bfloat16 [32, 4096, 1664], P('expert', 'dp')
- grad_router: float32 [1664, 32], replicated
Inputs may be any that keep to these rules, and one draw needn't show every extreme that they name: For each group and each expert, 32 distinct positions in increasing order; positions k * 128 to (k + 1) * 128 - 1 hold at most 2 of one expert's picks, and each expert takes exactly 2 from some such range in every group.
All inputs are finite; a program needn't handle non-finite values.
Results may differ from a plain program's by a relative error of at most 0.017.
Values may be sent and summed in bfloat16 or wider, within the bound.
No kernel may reach another device: no remote copies, remote signals or barrier semaphores. Data moves between devices by JAX's collectives and lax.ppermute only.
A program may use at most 64 MiB of HBM per device.

v0:
```python
import jax
import jax.numpy as jnp
from jax import lax
from jax.sharding import PartitionSpec as P

SLOT = 2


def normal_cdf(values):
    return 0.5 * (1.0 + jax.scipy.special.erf(values * 0.7071067811865476))


def gelu_exact(values):
    return values * normal_cdf(values)


def gelu_slope(values):
    return normal_cdf(values) + values * jnp.exp(-0.5 * values * values) * 0.3989422804014327


def contract_rows(left, right):
    return lax.dot_general(
        left, right, (((0,), (0,)), ((), ())), preferred_element_type=jnp.float32
    )


def contract_cols(left, right):
    return lax.dot_general(
        left, right, (((1,), (1,)), ((), ())), preferred_element_type=jnp.float32
    )


def shards(tokens, cotangent, counts, picks, router, w_in, w_out):
    experts = lax.axis_size("expert")
    owner_index = lax.axis_index("expert")
    tok_count = tokens.shape[0]
    feat_width = tokens.shape[1]
    pick_plan = picks[0]
    capacity = pick_plan.shape[1]
    bounds = jnp.arange(experts + 1, dtype=jnp.int32) * tok_count
    before = jnp.sum((pick_plan[:, :, None] < bounds[None, None, :]).astype(jnp.int32), axis=1)
    firsts = before[:, :experts]
    amounts = before[:, 1:] - firsts
    slot_rank = jnp.arange(SLOT, dtype=jnp.int32)
    own_first = lax.dynamic_index_in_dim(firsts, owner_index, 1, keepdims=False)
    own_amount = lax.dynamic_index_in_dim(amounts, owner_index, 1, keepdims=False)
    own_valid = slot_rank[None, :] < own_amount[:, None]
    own_pick = jnp.minimum(own_first[:, None] + slot_rank[None, :], capacity - 1)
    own_local = jnp.where(
        own_valid, jnp.take_along_axis(pick_plan, own_pick, axis=1) - owner_index * tok_count, 0
    )
    flat_local = own_local.reshape(-1)
    flat_valid = own_valid.reshape(-1)
    logits = jnp.dot(tokens.astype(jnp.float32), router, precision=lax.Precision.HIGHEST)
    router_prob = jax.nn.softmax(logits, axis=-1)
    weight = jnp.maximum(counts, 1).astype(jnp.float32)
    scaled = (cotangent.astype(jnp.float32) / weight[:, None]).astype(jnp.bfloat16)
    slot_keep = flat_valid[:, None]
    send_x = jnp.where(slot_keep, tokens[flat_local], 0).reshape(experts, SLOT, feat_width)
    send_dy = jnp.where(slot_keep, scaled[flat_local], 0).reshape(experts, SLOT, feat_width)
    expert_ids = jnp.arange(experts, dtype=jnp.int32)[:, None]
    send_gate = jnp.where(own_valid, router_prob[own_local, expert_ids], 0.0).astype(jnp.bfloat16)
    recv_x, recv_dy, recv_gate = (
        lax.all_to_all(send_x, "expert", split_axis=0, concat_axis=0, tiled=True),
        lax.all_to_all(send_dy, "expert", split_axis=0, concat_axis=0, tiled=True),
        lax.all_to_all(send_gate, "expert", split_axis=0, concat_axis=0, tiled=True),
    )
    slab_x = recv_x.reshape(experts * SLOT, feat_width)
    slab_dy = recv_dy.reshape(experts * SLOT, feat_width)
    slab_gate = recv_gate.reshape(-1)
    block_in = w_in[0]
    block_out = w_out[0]
    part_x = lax.all_gather(slab_x, "dp", axis=0, tiled=True)
    part_dy = lax.all_gather(slab_dy, "dp", axis=0, tiled=True)
    part_gate = lax.all_gather(slab_gate, "dp", axis=0, tiled=True)
    pre_act = jnp.dot(part_x, block_in, preferred_element_type=jnp.float32)
    activated = gelu_exact(pre_act).astype(jnp.bfloat16)
    part_out = jnp.dot(activated, block_out, preferred_element_type=jnp.float32)
    dy_wide = part_dy.astype(jnp.float32)
    gate_part = jnp.sum(dy_wide * part_out, axis=-1)
    out_grad = (part_gate.astype(jnp.float32)[:, None] * dy_wide).astype(jnp.bfloat16)
    act_grad = contract_cols(out_grad, block_out)
    pre_grad = (act_grad * gelu_slope(pre_act)).astype(jnp.bfloat16)
    row_part = contract_cols(pre_grad, block_in)
    grad_in = contract_rows(part_x, pre_grad)
    grad_out = contract_rows(activated, out_grad)
    rows_all = row_part
    gates_all = gate_part
    grad_in, grad_out, rows_all, gates_all = (grad_in, grad_out, rows_all, gates_all)
    row_sum = lax.psum_scatter(rows_all.astype(jnp.bfloat16), "dp", scatter_dimension=0, tiled=True)
    gate_sum = lax.psum_scatter(gates_all, "dp", scatter_dimension=0, tiled=True)
    gate_grad = gate_sum.astype(jnp.bfloat16)
    back_x = row_sum.reshape(experts, SLOT, feat_width)
    back_gate = gate_grad.reshape(experts, SLOT)
    ret_x, ret_gate = (
        lax.all_to_all(back_x, "expert", split_axis=0, concat_axis=0, tiled=True),
        lax.all_to_all(back_gate, "expert", split_axis=0, concat_axis=0, tiled=True),
    )
    token_ids = jnp.arange(tok_count, dtype=jnp.int32)
    hit_table = (flat_local[None, :] == token_ids[:, None]) & flat_valid[None, :]
    expert_sum = jnp.dot(
        hit_table.astype(jnp.bfloat16),
        ret_x.reshape(experts * SLOT, feat_width),
        preferred_element_type=jnp.float32,
    )
    gate_terms = jnp.where(flat_valid, ret_gate.reshape(-1).astype(jnp.float32), 0.0).reshape(
        experts, SLOT
    )
    hit_cube = hit_table.reshape(tok_count, experts, SLOT).astype(jnp.float32)
    prob_grad = jnp.einsum("tes,es->te", hit_cube, gate_terms, precision=lax.Precision.HIGHEST)
    logit_grad = router_prob * (
        prob_grad - jnp.sum(router_prob * prob_grad, axis=-1, keepdims=True)
    )
    grad_tokens = (
        expert_sum + jnp.dot(logit_grad, router.T, precision=lax.Precision.HIGHEST)
    ).astype(jnp.bfloat16)
    router_term = jnp.dot(tokens.astype(jnp.float32).T, logit_grad, precision=lax.Precision.HIGHEST)
    grad_router = lax.psum(router_term, ("dp", "expert"))
    return (
        grad_tokens,
        grad_in.astype(jnp.bfloat16)[None],
        grad_out.astype(jnp.bfloat16)[None],
        grad_router,
    )


def solution(mesh):
    placed = (
        P(("dp", "expert"), None),
        P(("dp", "expert"), None),
        P(("dp", "expert")),
        P("dp", None, None),
        P(),
        P("expert", None, "dp"),
        P("expert", "dp", None),
    )
    return jax.shard_map(
        shards,
        mesh=mesh,
        in_specs=placed,
        out_specs=(
            P(("dp", "expert"), None),
            P("expert", None, "dp"),
            P("expert", "dp", None),
            P(),
        ),
        check_vma=False,
    )
```

profile of v0, /device:TPU:1, one launch (start us, length us, event | category | flops | bytes accessed | tf_op | source)
XLA Modules:
  0.0 558.8 jit_solution(6839108845523890083)
XLA Ops:
  7.3 0.7 maximum_convert_fusion
  8.1 0.9 convert_reduce_fusion
  9.1 0.2 dynamic-slice_reduce_fusion
  9.4 0.1 lt.195
  9.9 0.8 gather_fusion.3
  10.8 0.2 copy-done.2
  10.9 0.8 gather_fusion.2
  11.8 0.1 divide_convert_fusion
  12.0 0.7 gather_fusion.1
  12.8 0.5 broadcast_select_fusion
  13.3 19.8 %all_to_all.31 = bf16[32,2,1664]{2,1,0:T(2,128)(2,1)S(1)} all-to-all(bf16[32,2,1664]{2,1,0:T(2,128)(2,1)S(1)} %get-tuple-element.10), channel_id=1, replica_groups=mesh['dp'=16,'expert'=32] {'expert'}, dimensions={0} | all-to-all | bytes 425984 | tf_op jit(solution)/shard_map/all_to_all | solution.py:64
  33.0 0.8 reshape.415
  33.9 14.9 %all_to_all.32 = bf16[32,2,1664]{2,1,0:T(2,128)(2,1)S(1)} all-to-all(bf16[32,2,1664]{2,1,0:T(2,128)(2,1)S(1)} %get-tuple-element.11), channel_id=1, replica_groups=mesh['dp'=16,'expert'=32] {'expert'}, dimensions={0} | all-to-all | bytes 425984 | tf_op jit(solution)/shard_map/all_to_all | solution.py:65
  48.8 0.8 reshape.414
  49.9 0.6 fusion.47
  51.3 0.6 fusion.48
  51.9 28.2 %all-gather.5.cloned.1.call-done = bf16[1024,1664]{1,0:T(8,128)(2,1)} async-done(((bf16[64,1664]{1,0:T(8,128)(2,1)}), bf16[1024,1664]{1,0:T(8,128)(2,1)}) %all-gather.5.cloned.1.call-update) | async-done | bytes 3407888 | tf_op jit(solution)/shard_map/all_gather | solution.py:73
  80.1 4.0 fusion.19
  84.1 41.3 %all-gather.3.cloned.1.call-done = bf16[1024,1664]{1,0:T(8,128)(2,1)} async-done(((bf16[64,1664]{1,0:T(8,128)(2,1)}), bf16[1024,1664]{1,0:T(8,128)(2,1)}) %all-gather.3.cloned.1.call-update) | async-done | bytes 3407888 | tf_op jit(solution)/shard_map/all_gather | solution.py:74
  125.4 3.5 fusion.1
  129.0 23.2 %all-reduce.1 = bf16[1024]{0:T(1024)(128)(2,1)S(1)} all-reduce(f32[1024]{0:T(1024)S(1)} %fusion.1), channel_id=3, replica_groups=mesh['dp'=16,'expert'=32] {'dp'}, use_global_device_ids=true, to_apply=%region_5.6.clone | all-reduce | flops 1024 | bytes 6144
  152.2 0.7 all_to_all.25
  153.0 9.3 %all-to-all-start.4 = ((bf16[32,1,2]{2,1,0:T(2,128)(2,1)}), bf16[32,1,2]{2,1,0:T(2,128)(2,1)S(1)}, u32[]{:S(2)}, u32[]{:S(2)}) async-start(bf16[32,1,2]{2,1,0:T(2,128)(2,1)} %all_to_all.25), calls=%async_computation.5 | async-start | bytes 32768 | tf_op jit(solution)/shard_map/all_to_all | solution.py:97
  162.4 8.5 %all-to-all-done.4 = bf16[32,1,2]{2,1,0:T(2,128)(2,1)S(1)} async-done(((bf16[32,1,2]{2,1,0:T(2,128)(2,1)}), bf16[32,1,2]{2,1,0:T(2,128)(2,1)S(1)}, u32[]{:S(2)}, u32[]{:S(2)}) %all-to-all-start.4) | async-done | bytes 160 | tf_op jit(solution)/shard_map/all_to_all | solution.py:97
  171.0 0.2 fusion.26
  171.3 0.8 gather_fusion
  172.1 0.1 gather.29
  172.3 0.7 copy.61
  173.0 3.8 all-to-all-start
  177.6 7.9 %all-to-all-done = bf16[32,1,2]{2,1,0:T(2,128)(2,1)S(1)} async-done(((bf16[32,1,2]{2,1,0:T(2,128)(2,1)}), bf16[32,1,2]{2,1,0:T(2,128)(2,1)S(1)}, u32[]{:S(2)}, u32[]{:S(2)}) %all-to-all-start) | async-done | bytes 160 | tf_op jit(solution)/shard_map/all_to_all | solution.py:66
  185.5 0.1 reshape.451
  185.7 0.2 dynamic-update-slice
  185.9 27.7 %all-reduce = bf16[1024]{0:T(1024)(128)(2,1)S(1)} all-reduce(bf16[1024]{0:T(1024)(128)(2,1)S(1)} %dynamic-update-slice), channel_id=1, replica_groups=mesh['dp'=16,'expert'=32] {'dp'}, use_global_device_ids=true, to_apply=%add | all-reduce | flops 1024 | bytes 4096
  213.6 3.6 fusion.11
  217.2 2.9 convolution_convert_fusion
  220.1 0.2 all-reduce.4.cloned.1.call-start
  220.4 0.1 lt.180
  220.7 1.0 convolution_bitcast_fusion
  221.7 4.1 fusion.2
  225.8 49.4 %reduce-scatter.2.cloned.1.call-done = bf16[64,1664]{1,0:T(8,128)(2,1)} async-done(((bf16[1024,1664]{1,0:T(8,128)(2,1)}), bf16[64,1664]{1,0:T(8,128)(2,1)}) %reduce-scatter.2.cloned.1.call-update) | async-done | bytes 213008 | tf_op jit(solution)/shard_map/reduce_scatter | solution.py:90
  275.1 1.7 reshape.416
  276.8 9.1 %all-to-all-start.3 = ((bf16[32,2,1664]{2,1,0:T(2,128)(2,1)}), bf16[32,2,1664]{2,1,0:T(2,128)(2,1)S(1)}, u32[]{:S(2)}, u32[]{:S(2)}) async-start(bf16[32,2,1664]{2,1,0:T(2,128)(2,1)} %reshape.416), calls=%async_computation.4 | async-start | bytes 425984 | tf_op jit(solution)/shard_map/all_to_all | solution.py:96
  285.9 4.1 fusion.3
  290.1 5.3 all-to-all-done.3
  295.5 0.3 fusion.24
  295.7 1.7 fusion.4
  297.4 253.2 %all-reduce.4.cloned.1.call-done = f32[1664,32]{0,1:T(8,128)} async-done(((f32[1664,32]{0,1:T(8,128)}), f32[1664,32]{0,1:T(8,128)}) %all-reduce.4.cloned.1.call-update) | async-done | bytes 213008 | tf_op jit(solution)/shard_map/psum | solution.py:118
  550.6 1.6 copy.76
  (59 shorter events, 2.4 us)
Async XLA Ops:
  7.2 72.9 %copy-start = (bf16[1,1664,256]{2,1,0:T(8,128)(2,1)S(1)}, bf16[1,1664,256]{2,1,0:T(8,128)(2,1)}, u32[]{:S(2)}) copy-start(bf16[1,1664,256]{2,1,0:T(8,128)(2,1)} %param.12) | copy-start | bytes 2555908
  7.2 2.7 copy-start.1
  7.2 72.9 %all-gather.5.cloned.1.call-start = ((), (), s32[]{:S(2)}) async-start(), calls=%async_computation.7 | async-start | bytes 3620864 | tf_op jit(solution)/shard_map/all_gather | solution.py:73
  9.9 1.0 copy-start.2
  9.9 1.9 copy-start.4
  11.7 38.2 %copy-start.5 = (u32[512]{0:T(512)S(1)}, u32[512]{0:T(512)}, u32[]{:S(2)}) copy-start(u32[512]{0:T(512)} %constant.91) | copy-start | bytes 6148
  11.7 39.6 %copy-start.3 = (f32[1664,32]{0,1:T(8,128)S(1)}, f32[1664,32]{0,1:T(8,128)}, u32[]{:S(2)}) copy-start(f32[1664,32]{0,1:T(8,128)} %param.11) | copy-start | bytes 638980
  33.8 91.6 %all-gather.3.cloned.1.call-start = ((), (), s32[]{:S(2)}) async-start(), calls=%async_computation.6 | async-start | bytes 3620864 | tf_op jit(solution)/shard_map/all_gather | solution.py:74
  51.9 73.5 %copy-start.6 = (bf16[1,256,1664]{2,1,0:T(8,128)(2,1)S(1)}, bf16[1,256,1664]{2,1,0:T(8,128)(2,1)}, u32[]{:S(2)}) copy-start(bf16[1,256,1664]{2,1,0:T(8,128)(2,1)} %param.13) | copy-start | bytes 2555908
  153.0 17.9 %all-to-all-start.4 = ((bf16[32,1,2]{2,1,0:T(2,128)(2,1)}), bf16[32,1,2]{2,1,0:T(2,128)(2,1)S(1)}, u32[]{:S(2)}, u32[]{:S(2)}) async-start(bf16[32,1,2]{2,1,0:T(2,128)(2,1)} %all_to_all.25), calls=%async_computation.5 | async-start | bytes 32768 | tf_op jit(solution)/shard_map/all_to_all | solution.py:97
  173.0 12.4 %all-to-all-start = ((bf16[32,1,2]{2,1,0:T(2,128)(2,1)}), bf16[32,1,2]{2,1,0:T(2,128)(2,1)S(1)}, u32[]{:S(2)}, u32[]{:S(2)}) async-start(bf16[32,1,2]{2,1,0:T(2,128)(2,1)} %copy.61), calls=%async_computation | async-start | bytes 32768 | tf_op jit(solution)/shard_map/all_to_all | solution.py:66
  176.9 98.3 %reduce-scatter.2.cloned.1.call-start = ((), (), s32[]{:S(2)}) async-start(), calls=%async_computation.8 | async-start | bytes 3620864 | tf_op jit(solution)/shard_map/reduce_scatter | solution.py:90
  220.1 330.5 %all-reduce.4.cloned.1.call-start = ((), (), s32[]{:S(2)}) async-start(), calls=%async_computation.9 | async-start | bytes 425984 | tf_op jit(solution)/shard_map/psum | solution.py:118
  221.7 64.2 %copy-start.7 = (f32[1024,256]{1,0:T(8,128)S(1)}, f32[1024,256]{1,0:T(8,128)}, u32[]{:S(2)}) copy-start(f32[1024,256]{1,0:T(8,128)} %fusion.19) | copy-start | bytes 3145732
  276.8 18.5 %all-to-all-start.3 = ((bf16[32,2,1664]{2,1,0:T(2,128)(2,1)}), bf16[32,2,1664]{2,1,0:T(2,128)(2,1)S(1)}, u32[]{:S(2)}, u32[]{:S(2)}) async-start(bf16[32,2,1664]{2,1,0:T(2,128)(2,1)} %reshape.416), calls=%async_computation.4 | async-start | bytes 425984 | tf_op jit(solution)/shard_map/all_to_all | solution.py:96
Sparse Core Ops, SparseCore 0:
  33.9 46.0 all-gather.4
  82.8 42.5 all-gather.2
  220.3 54.8 reduce-scatter.1
  280.0 270.5 all-reduce.3
where the time goes:
time: 559 us
  waiting for transfers between devices  394 us (70%)
  blocking collectives  85.6 us (15%)
  matrix products  26 us (5%)
  starting transfers between devices  22.5 us (4%)
  between operations  15.4 us (3%)
  local copies, waits for them, and re-layouts  12.6 us (2%)
    psum x1, waiting for transfers between devices, shards(): grad_router = lax.psum(router_term, ('dp', 'expert'))  253 us
    unnamed x2, blocking collectives  50.9 us
    reduce_scatter x1, waiting for transfers between devices, shards(): lax.psum_scatter(rows_all.astype(jnp.bfloat16), 'dp', scatter_dimension=0...  49.4 us
    all_gather x1, waiting for transfers between devices, shards(): part_dy = lax.all_gather(slab_dy, 'dp', axis=0, tiled=True)  41.3 us
    all_gather x1, waiting for transfers between devices, shards(): part_x = lax.all_gather(slab_x, 'dp', axis=0, tiled=True)  28.2 us
    all_to_all x1, blocking collectives, shards(): lax.all_to_all(send_x, 'expert', split_axis=0, concat_axis=0, tiled=True)  19.8 us
    all_to_all x1, blocking collectives, shards(): lax.all_to_all(send_dy, 'expert', split_axis=0, concat_axis=0, tiled=True)  14.9 us
  transfers between devices with their start and end apart: 7, of which 7 were waited for; matrix products, arithmetic and copies ran while one was open for 4% of the time, Pallas kernels for 0%

commit v1 on v0

--- a/solution.py
+++ b/solution.py
@@ -71,7 +71,10 @@
     block_in = w_in[0]
     block_out = w_out[0]
     part_x = lax.all_gather(slab_x, "dp", axis=0, tiled=True)
-    part_dy = lax.all_gather(slab_dy, "dp", axis=0, tiled=True)
+    size = lax.axis_size("dp")
+    blocks = jnp.stack([slab_dy for _ in range(size)])
+    blocks = lax.all_to_all(blocks, "dp", split_axis=0, concat_axis=0)
+    part_dy = jnp.concatenate(blocks, axis=0)
     part_gate = lax.all_gather(slab_gate, "dp", axis=0, tiled=True)
     pre_act = jnp.dot(part_x, block_in, preferred_element_type=jnp.float32)
     activated = gelu_exact(pre_act).astype(jnp.bfloat16)

time: 559 us -> 586 us (1.048)
  waiting for transfers between devices: 394 us -> 416 us
  starting transfers between devices: 22.5 us -> 38 us
  blocking collectives: 85.6 us -> 70.2 us
  other arithmetic: 2.9 us -> 10.1 us
    all_gather x1 -> x0, waiting for transfers between devices: 41.3 us -> none  [shards(): part_dy = lax.all_gather(slab_dy, 'dp', axis=0, tiled=True)]
    all_gather x1, waiting for transfers between devices: 28.2 us -> 66.8 us  [shards(): part_x = lax.all_gather(slab_x, 'dp', axis=0, tiled=True)]
    all_to_all x0 -> x2, waiting for transfers between devices: none -> 26.6 us  [the longest x1 18 us: shards(): blocks = lax.all_to_all(blocks, 'dp', split_axis=0, concat_axis=0)]
    all_to_all x0 -> x2, starting transfers between devices: none -> 19.2 us  [the longest x1 13.6 us: shards(): blocks = lax.all_to_all(blocks, 'dp', split_axis=0, concat_axis=0)]
    all_to_all x1 -> x0, blocking collectives: 14.9 us -> none  [shards(): lax.all_to_all(send_dy, 'expert', split_axis=0, concat_axis=0, tiled=True)]
    convert_element_type x0 -> x2, other arithmetic: none -> 7.18 us  [shards(): (part_gate.astype(jnp.float32)[:, None] * dy_wide).astype(jnp.bfloat16)]
  transfers between devices with their start and end apart: 7 -> 8, of which waited for: 7 -> 8; matrix products, arithmetic and copies ran while one was open for 4% -> 4% of each run, Pallas kernels for 0% -> 0%
where the time goes in v1:
time: 586 us
  waiting for transfers between devices  416 us (71%)
  blocking collectives  70.2 us (12%)
  starting transfers between devices  38 us (6%)
  matrix products  21.7 us (4%)
  between operations  15.4 us (3%)
  local copies, waits for them, and re-layouts  14 us (2%)
  other arithmetic  10.1 us (2%)
    psum x1, waiting for transfers between devices, shards(): grad_router = lax.psum(router_term, ('dp', 'expert'))  253 us
    all_gather x1, waiting for transfers between devices, shards(): part_x = lax.all_gather(slab_x, 'dp', axis=0, tiled=True)  66.8 us
    unnamed x2, blocking collectives  50.5 us
    reduce_scatter x1, waiting for transfers between devices, shards(): lax.psum_scatter(rows_all.astype(jnp.bfloat16), 'dp', scatter_dimension=0...  50.1 us
    all_to_all x1, blocking collectives, shards(): lax.all_to_all(send_x, 'expert', split_axis=0, concat_axis=0, tiled=True)  19.8 us
    all_to_all x1, waiting for transfers between devices, shards(): blocks = lax.all_to_all(blocks, 'dp', split_axis=0, concat_axis=0)  18 us
    all_to_all x1, starting transfers between devices, shards(): blocks = lax.all_to_all(blocks, 'dp', split_axis=0, concat_axis=0)  13.6 us
  transfers between devices with their start and end apart: 8, of which 8 were waited for; matrix products, arithmetic and copies ran while one was open for 4% of the time, Pallas kernels for 0%

profile of v1, /device:TPU:1, one launch (start us, length us, event | category | flops | bytes accessed | tf_op | source)
XLA Modules:
  0.0 585.8 jit_solution(18219399909320007648)
XLA Ops:
  7.2 1.0 convert_reduce_fusion
  8.3 0.2 dynamic-slice_reduce_fusion
  8.6 0.1 lt.195
  9.0 0.8 gather_fusion.3
  10.1 0.8 gather_fusion.2
  11.0 0.1 divide_convert_fusion
  11.1 0.8 gather_fusion.1
  12.0 1.1 broadcast_select_fusion
  13.1 19.8 %all_to_all.36 = bf16[32,2,1664]{2,1,0:T(2,128)(2,1)S(1)} all-to-all(bf16[32,2,1664]{2,1,0:T(2,128)(2,1)S(1)} %get-tuple-element.10), channel_id=1, replica_groups=mesh['dp'=16,'expert'=32] {'expert'}, dimensions={0} | all-to-all | bytes 425984 | tf_op jit(solution)/shard_map/all_to_all | solution.py:64
  32.9 5.6 all-to-all-start.1
  38.6 0.8 reshape.422
  39.4 8.6 %all-to-all-done.1 = bf16[32,2,1664]{2,1,0:T(2,128)(2,1)S(1)} async-done(((bf16[32,2,1664]{2,1,0:T(2,128)(2,1)}), bf16[32,2,1664]{2,1,0:T(2,128)(2,1)S(1)}, u32[]{:S(2)}, u32[]{:S(2)}) %all-to-all-start.1) | async-done | bytes 213024 | tf_op jit(solution)/shard_map/all_to_all | solution.py:65
  48.1 2.1 stack.3
  50.2 13.6 %all-to-all-start.2 = ((bf16[16,64,1664]{2,1,0:T(8,128)(2,1)}), bf16[16,64,1664]{2,1,0:T(8,128)(2,1)}, u32[]{:S(2)}, u32[]{:S(2)}) async-start(bf16[16,64,1664]{2,1,0:T(8,128)(2,1)} %stack.3), calls=%async_computation.2 | async-start | bytes 6815744 | tf_op jit(solution)/shard_map/all_to_all | solution.py:76
  64.1 0.6 fusion.40
  65.6 0.6 fusion.41
  66.1 66.8 %all-gather.2.cloned.1.call-done = bf16[1024,1664]{1,0:T(8,128)(2,1)} async-done(((bf16[64,1664]{1,0:T(8,128)(2,1)}), bf16[1024,1664]{1,0:T(8,128)(2,1)}) %all-gather.2.cloned.1.call-update) | async-done | bytes 3407888 | tf_op jit(solution)/shard_map/all_gather | solution.py:73
  132.9 4.0 fusion.12
  136.9 18.0 %all-to-all-done.2 = bf16[16,64,1664]{2,1,0:T(8,128)(2,1)} async-done(((bf16[16,64,1664]{2,1,0:T(8,128)(2,1)}), bf16[16,64,1664]{2,1,0:T(8,128)(2,1)}, u32[]{:S(2)}, u32[]{:S(2)}) %all-to-all-start.2) | async-done | bytes 3407904 | tf_op jit(solution)/shard_map/all_to_all | solution.py:76
  155.0 3.5 fusion.1
  158.5 23.5 %all-reduce.1 = bf16[1024]{0:T(1024)(128)(2,1)S(1)} all-reduce(f32[1024]{0:T(1024)S(1)} %fusion.1), channel_id=3, replica_groups=mesh['dp'=16,'expert'=32] {'dp'}, use_global_device_ids=true, to_apply=%region_5.6.clone | all-reduce | flops 1024 | bytes 6144
  182.1 0.7 all_to_all.29
  182.9 5.6 all-to-all-start.5
  188.6 8.5 %all-to-all-done.5 = bf16[32,1,2]{2,1,0:T(2,128)(2,1)S(1)} async-done(((bf16[32,1,2]{2,1,0:T(2,128)(2,1)}), bf16[32,1,2]{2,1,0:T(2,128)(2,1)S(1)}, u32[]{:S(2)}, u32[]{:S(2)}) %all-to-all-start.5) | async-done | bytes 160 | tf_op jit(solution)/shard_map/all_to_all | solution.py:100
  197.3 0.2 fusion.19
  197.5 0.8 gather_fusion
  198.6 0.7 copy.61
  199.3 3.8 all-to-all-start
  203.8 7.9 %all-to-all-done = bf16[32,1,2]{2,1,0:T(2,128)(2,1)S(1)} async-done(((bf16[32,1,2]{2,1,0:T(2,128)(2,1)}), bf16[32,1,2]{2,1,0:T(2,128)(2,1)S(1)}, u32[]{:S(2)}, u32[]{:S(2)}) %all-to-all-start) | async-done | bytes 160 | tf_op jit(solution)/shard_map/all_to_all | solution.py:66
  211.8 0.1 reshape.459
  211.9 0.2 dynamic-update-slice
  212.1 26.9 %all-reduce = bf16[1024]{0:T(1024)(128)(2,1)S(1)} all-reduce(bf16[1024]{0:T(1024)(128)(2,1)S(1)} %dynamic-update-slice), channel_id=1, replica_groups=mesh['dp'=16,'expert'=32] {'dp'}, use_global_device_ids=true, to_apply=%add | all-reduce | flops 1024 | bytes 4096
  239.1 2.7 fusion
  241.8 1.3 fusion.6
  243.1 2.9 convolution_convert_fusion
  246.1 0.2 all-reduce.4.cloned.1.call-start
  246.7 1.0 convolution_bitcast_fusion
  247.7 4.5 fusion.2
  252.2 50.1 %reduce-scatter.2.cloned.1.call-done = bf16[64,1664]{1,0:T(8,128)(2,1)} async-done(((bf16[1024,1664]{1,0:T(8,128)(2,1)}), bf16[64,1664]{1,0:T(8,128)(2,1)}) %reduce-scatter.2.cloned.1.call-update) | async-done | bytes 213008 | tf_op jit(solution)/shard_map/reduce_scatter | solution.py:93
  302.3 1.7 reshape.423
  304.0 9.0 %all-to-all-start.4 = ((bf16[32,2,1664]{2,1,0:T(2,128)(2,1)}), bf16[32,2,1664]{2,1,0:T(2,128)(2,1)S(1)}, u32[]{:S(2)}, u32[]{:S(2)}) async-start(bf16[32,2,1664]{2,1,0:T(2,128)(2,1)} %reshape.423), calls=%async_computation.5 | async-start | bytes 425984 | tf_op jit(solution)/shard_map/all_to_all | solution.py:99
  313.1 4.2 fusion.4
  317.2 2.0 fusion.3
  319.2 3.2 all-to-all-done.4
  322.6 0.2 fusion.17
  322.8 1.7 fusion.5
  324.5 253.2 %all-reduce.4.cloned.1.call-done = f32[1664,32]{0,1:T(8,128)} async-done(((f32[1664,32]{0,1:T(8,128)}), f32[1664,32]{0,1:T(8,128)}) %all-reduce.4.cloned.1.call-update) | async-done | bytes 213008 | tf_op jit(solution)/shard_map/psum | solution.py:121
  577.7 1.6 copy.76
  (69 shorter events, 2.7 us)
Async XLA Ops:
  7.2 125.7 %copy-start = (bf16[1,1664,256]{2,1,0:T(8,128)(2,1)S(1)}, bf16[1,1664,256]{2,1,0:T(8,128)(2,1)}, u32[]{:S(2)}) copy-start(bf16[1,1664,256]{2,1,0:T(8,128)(2,1)} %param.12) | copy-start | bytes 2555908
  7.2 1.7 copy-start.1
  8.9 1.2 copy-start.2
  8.9 2.0 copy-start.8
  8.9 2.0 copy-start.4
  32.9 15.1 %all-to-all-start.1 = ((bf16[32,2,1664]{2,1,0:T(2,128)(2,1)}), bf16[32,2,1664]{2,1,0:T(2,128)(2,1)S(1)}, u32[]{:S(2)}, u32[]{:S(2)}) async-start(bf16[32,2,1664]{2,1,0:T(2,128)(2,1)} %get-tuple-element.11), calls=%async_computation.1 | async-start | bytes 425984 | tf_op jit(solution)/shard_map/all_to_all | solution.py:65
  38.5 94.4 %all-gather.2.cloned.1.call-start = ((), (), s32[]{:S(2)}) async-start(), calls=%async_computation.7 | async-start | bytes 3620864 | tf_op jit(solution)/shard_map/all_gather | solution.py:73
  50.2 13.9 %copy-start.5 = (u32[512]{0:T(512)S(1)}, u32[512]{0:T(512)}, u32[]{:S(2)}) copy-start(u32[512]{0:T(512)} %constant.91) | copy-start | bytes 6148
  50.2 15.4 %copy-start.3 = (f32[1664,32]{0,1:T(8,128)S(1)}, f32[1664,32]{0,1:T(8,128)}, u32[]{:S(2)}) copy-start(f32[1664,32]{0,1:T(8,128)} %param.11) | copy-start | bytes 638980
  50.2 104.8 %all-to-all-start.2 = ((bf16[16,64,1664]{2,1,0:T(8,128)(2,1)}), bf16[16,64,1664]{2,1,0:T(8,128)(2,1)}, u32[]{:S(2)}, u32[]{:S(2)}) async-start(bf16[16,64,1664]{2,1,0:T(8,128)(2,1)} %stack.3), calls=%async_computation.2 | async-start | bytes 6815744 | tf_op jit(solution)/shard_map/all_to_all | solution.py:76
  66.1 88.8 %copy-start.7 = (bf16[1,256,1664]{2,1,0:T(8,128)(2,1)S(1)}, bf16[1,256,1664]{2,1,0:T(8,128)(2,1)}, u32[]{:S(2)}) copy-start(bf16[1,256,1664]{2,1,0:T(8,128)(2,1)} %param.13) | copy-start | bytes 2555908
  182.9 14.2 %all-to-all-start.5 = ((bf16[32,1,2]{2,1,0:T(2,128)(2,1)}), bf16[32,1,2]{2,1,0:T(2,128)(2,1)S(1)}, u32[]{:S(2)}, u32[]{:S(2)}) async-start(bf16[32,1,2]{2,1,0:T(2,128)(2,1)} %all_to_all.29), calls=%async_computation.6 | async-start | bytes 32768 | tf_op jit(solution)/shard_map/all_to_all | solution.py:100
  199.3 12.4 %all-to-all-start = ((bf16[32,1,2]{2,1,0:T(2,128)(2,1)}), bf16[32,1,2]{2,1,0:T(2,128)(2,1)S(1)}, u32[]{:S(2)}, u32[]{:S(2)}) async-start(bf16[32,1,2]{2,1,0:T(2,128)(2,1)} %copy.61), calls=%async_computation | async-start | bytes 32768 | tf_op jit(solution)/shard_map/all_to_all | solution.py:66
  203.1 99.2 %reduce-scatter.2.cloned.1.call-start = ((), (), s32[]{:S(2)}) async-start(), calls=%async_computation.8 | async-start | bytes 3620864 | tf_op jit(solution)/shard_map/reduce_scatter | solution.py:93
  239.1 2.7 copy-start.9
  246.1 331.6 %all-reduce.4.cloned.1.call-start = ((), (), s32[]{:S(2)}) async-start(), calls=%async_computation.9 | async-start | bytes 425984 | tf_op jit(solution)/shard_map/psum | solution.py:121
  247.7 65.3 %copy-start.10 = (f32[1024,256]{1,0:T(8,128)S(1)}, f32[1024,256]{1,0:T(8,128)}, u32[]{:S(2)}) copy-start(f32[1024,256]{1,0:T(8,128)} %fusion.12) | copy-start | bytes 3145732
  304.0 18.5 %all-to-all-start.4 = ((bf16[32,2,1664]{2,1,0:T(2,128)(2,1)}), bf16[32,2,1664]{2,1,0:T(2,128)(2,1)S(1)}, u32[]{:S(2)}, u32[]{:S(2)}) async-start(bf16[32,2,1664]{2,1,0:T(2,128)(2,1)} %reshape.423), calls=%async_computation.5 | async-start | bytes 425984 | tf_op jit(solution)/shard_map/all_to_all | solution.py:99
  313.0 4.2 copy-start.6
Sparse Core Ops, SparseCore 0:
  42.0 90.8 all-gather.1
  246.2 56.0 reduce-scatter.1
  307.3 270.3 all-reduce.3
